TPU v7x, 32 devices: a whole 2x2x4 slice. The times are simulated.
32 devices in a mesh: rows: 8 (over y, x, core), heads: 4 (over z).
Axes of the slice: x: 2, y: 2, z: 4, core: 2. Of those that a mesh axis runs over, the one named last changes fastest.
Arguments:
- test_rows: bfloat16 [1024, 512], P('rows'), may hold values from -6 to 6
- query_weight: bfloat16 [512, 512], P(None, 'heads'), may hold values from -0.54120401 to 0.54120401
- keys: bfloat16 [32768, 512], P('rows', 'heads'), may hold values from -8 to 8
- values: bfloat16 [32768, 512], P('rows', 'heads'), may hold values from -6 to 6
- out_weight: bfloat16 [512, 512], P('heads'), may hold values from -0.25 to 0.25
Outputs:
- mixed: bfloat16 [1024, 512], P('rows', 'heads')
All inputs are finite; a program needn't handle non-finite values.
Results may differ from a plain program's by a relative error of at most 0.0079.
Values may be sent and summed in bfloat16 or wider, within the bound.
A program may use at most 64 MiB of HBM per device.

v0:
```python
import functools
import math

import jax
import jax.numpy as jnp
from jax import lax
from jax.experimental import pallas as pl
from jax.experimental.pallas import tpu as pltpu
from jax.sharding import PartitionSpec as P

HEAD_DIM = 64
LOG2E = math.log2(math.e)
MESH = pl.DeviceIdType.MESH
CHUNK = 512


def xor_of(a, b, count):
    total = 0
    bit = 1
    while bit < count:
        one = (a // bit) % 2
        two = (b // bit) % 2
        total = total + bit * (one + two - 2 * one * two)
        bit *= 2
    return total


def peer_of(me, step, count):
    other = ((step - 1) * (step - 1) + count * count - 1) // (count * count)
    early = ((count - 1 - step) * (count - 1 - step) + count * count - 1) // (count * count)
    mask = other * early * (count + 1 - step) + 2 * (1 - other) + (1 - early)
    return xor_of(me, mask, count)


def kernel(
    n, nz, chunk,
    x_hbm, wq_hbm, k_hbm, v_hbm, wo_hbm, o_ref,
    x_ref, wq_ref, k_ref, v_ref, wo_ref, vt_ref, qall, s0, s1,
    num_out, stat_out, num_in, stat_in, att, wo_in,
    in_sem, q_send, q_recv, n_send, n_recv, t_send, t_recv, a_send, a_recv, w_send, w_recv,
):
    me = lax.axis_index("rows")
    mz = lax.axis_index("heads")
    count = x_ref.shape[0]
    ctx, width = k_ref.shape
    cols = o_ref.shape[1]
    f32, bf = jnp.float32, jnp.bfloat16
    chunks = [pl.ds(c, chunk) for c in range(0, ctx, chunk)]

    loads = [
        pltpu.make_async_copy(src, dst, in_sem.at[i])
        for i, (src, dst) in enumerate([
            (x_hbm, x_ref), (wq_hbm, wq_ref), (k_hbm, k_ref), (v_hbm, v_ref), (wo_hbm, wo_ref)])]
    for load in loads:
        load.start()

    barrier = pltpu.get_barrier_semaphore()
    for i in range(1, n):
        pl.semaphore_signal(barrier, inc=1, device_id={"rows": xor_of(me, i, n)}, device_id_type=MESH)
    for i in range(1, nz):
        pl.semaphore_signal(barrier, inc=1, device_id={"heads": (mz + i) % nz}, device_id_type=MESH)

    loads[0].wait()
    loads[1].wait()
    q = jnp.dot(x_ref[...], wq_ref[...], preferred_element_type=f32).astype(bf)
    qall[me] = q * jnp.bfloat16(HEAD_DIM ** -0.5)

    pl.semaphore_wait(barrier, n - 1 + nz - 1)

    def q_copy(peer, slot):
        return pltpu.make_async_remote_copy(
            src_ref=qall.at[me], dst_ref=qall.at[slot], send_sem=q_send.at[peer],
            recv_sem=q_recv.at[slot], device_id={"rows": peer}, device_id_type=MESH)

    def w_copy(i):
        peer = (mz + i) % nz
        return pltpu.make_async_remote_copy(
            src_ref=wo_ref.at[:, pl.ds(pl.multiple_of(peer * cols, cols), cols)],
            dst_ref=wo_in.at[mz], send_sem=w_send.at[i], recv_sem=w_recv.at[mz],
            device_id={"heads": peer}, device_id_type=MESH)

    for i in range(1, n):
        q_copy(peer_of(me, i, n), me).start()
    loads[4].wait()
    for i in range(1, nz):
        w_copy(i).start()

    lane = lax.broadcasted_iota(jnp.int32, (1, width), 1)
    keep0 = jnp.where(lane < HEAD_DIM, 1.0, 0.0).astype(bf)
    keep1 = jnp.where(lane < HEAD_DIM, 0.0, 1.0).astype(bf)

    def both_heads(peer):
        q = qall[peer]
        return jnp.concatenate([q * keep0, q * keep1], axis=0)

    def score(both, part, s_ref, top):
        s = lax.dot_general(k_ref[part, :], both, (((1,), (1,)), ((), ())), preferred_element_type=f32)
        s_ref[part, :] = s
        here = jnp.max(s, axis=0, keepdims=True)
        return here if top is None else jnp.maximum(top, here)

    def weigh(s_ref, part, top, total, acc):
        w = jnp.exp2((s_ref[part, :] - top) * LOG2E)
        here = jnp.sum(w, axis=0, keepdims=True)
        summed = jnp.dot(vt_ref[:, part], w.astype(bf), preferred_element_type=f32)
        return (here, summed) if total is None else (total + here, acc + summed)

    def keep(peer, top, total, acc):
        num = jnp.concatenate([acc[:HEAD_DIM, :count], acc[HEAD_DIM:, count:]], axis=0)
        num_out[peer] = num.astype(num_out.dtype)
        stat_out[peer, 0:1, :] = top[:, :count]
        stat_out[peer, 1:2, :] = top[:, count:]
        stat_out[peer, 2:3, :] = total[:, :count]
        stat_out[peer, 3:4, :] = total[:, count:]

    def turn(now, s_now, top, later, s_later):
        both = None if later is None else both_heads(later)
        after = total = acc = None
        for part in chunks:
            if both is not None:
                after = score(both, part, s_later, after)
            total, acc = weigh(s_now, part, top, total, acc)
        keep(now, top, total, acc)
        return after

    def n_copy(peer, slot):
        return pltpu.make_async_remote_copy(
            src_ref=num_out.at[peer], dst_ref=num_in.at[slot], send_sem=n_send.at[peer],
            recv_sem=n_recv.at[slot], device_id={"rows": peer}, device_id_type=MESH)

    def t_copy(peer, slot):
        return pltpu.make_async_remote_copy(
            src_ref=stat_out.at[peer], dst_ref=stat_in.at[slot], send_sem=t_send.at[peer],
            recv_sem=t_recv.at[slot], device_id={"rows": peer}, device_id_type=MESH)

    def send(peer):
        n_copy(peer, me).start()
        t_copy(peer, me).start()

    def await_q(step):
        peer = peer_of(me, step, n)
        q_copy(peer, peer).wait_recv()
        return peer

    stat_out[...] = jnp.zeros(stat_out.shape, f32)
    loads[2].wait()
    loads[3].wait()
    both = both_heads(me)
    top = None
    for part in chunks:
        top = score(both, part, s0, top)
        vt_ref[:, part] = v_ref[part, :].T

    top = turn(me, s0, top, await_q(1), s1)

    def two(pair, top):
        step = 2 * pair + 1
        now, later = peer_of(me, step, n), await_q(step + 1)
        top = turn(now, s1, top, later, s0)
        send(now)
        now, later = later, await_q(step + 2)
        top = turn(now, s0, top, later, s1)
        send(now)
        return top

    top = lax.fori_loop(0, (n - 2) // 2, two, top)
    last = peer_of(me, n - 1, n)
    turn(last, s1, top, None, None)
    send(last)

    def parts(peer, num_ref, stat_ref):
        return (num_ref[peer].astype(f32), stat_ref[peer, 0:2, :], stat_ref[peer, 2:4, :])

    def spread(pair):
        return jnp.concatenate([
            jnp.broadcast_to(pair[0:1, :], (HEAD_DIM, count)),
            jnp.broadcast_to(pair[1:2, :], (HEAD_DIM, count))], axis=0)

    def merge(step, state):
        num, m, l = state
        peer = peer_of(me, step, n)
        n_copy(peer, peer).wait_recv()
        t_copy(peer, peer).wait_recv()
        num2, m2, l2 = parts(peer, num_in, stat_in)
        top = jnp.maximum(m, m2)
        a = jnp.exp2((m - top) * LOG2E)
        b = jnp.exp2((m2 - top) * LOG2E)
        return num * spread(a) + num2 * spread(b), top, l * a + l2 * b

    num, m, l = lax.fori_loop(1, n, merge, parts(me, num_out, stat_out))
    att[mz] = (num / spread(l)).T.astype(bf)

    def a_copy(i, slot):
        return pltpu.make_async_remote_copy(
            src_ref=att.at[mz], dst_ref=att.at[slot], send_sem=a_send.at[i],
            recv_sem=a_recv.at[slot], device_id={"heads": (mz + i) % nz}, device_id_type=MESH)

    for i in range(1, nz):
        a_copy(i, mz).start()
    for i in range(1, nz):
        z = (mz + i) % nz
        pltpu.make_async_remote_copy(
            src_ref=wo_ref.at[:, pl.ds(0, cols)], dst_ref=wo_in.at[z], send_sem=w_send.at[i],
            recv_sem=w_recv.at[z], device_id={"heads": z}, device_id_type=MESH).wait_recv()
    for i in range(1, n):
        peer = peer_of(me, i, n)
        q_copy(peer, me).wait_send()
        n_copy(peer, me).wait_send()
        t_copy(peer, me).wait_send()
    for i in range(1, nz):
        w_copy(i).wait_send()
    out = jnp.dot(att[mz], wo_ref[:, pl.ds(pl.multiple_of(mz * cols, cols), cols)],
                  preferred_element_type=f32)
    for i in range(1, nz):
        z = (mz + i) % nz
        a_copy(i, z).wait_recv()
        out += jnp.dot(att[z], wo_in[z], preferred_element_type=f32)
    o_ref[...] = out.astype(o_ref.dtype)
    for i in range(1, nz):
        a_copy(i, mz).wait_send()


def shards(n, nz, test_rows, query_weight, keys, values, out_weight):
    count, depth = test_rows.shape
    ctx, width = keys.shape
    cols = out_weight.shape[1] // nz
    bf, f32 = jnp.bfloat16, jnp.float32
    dma = pltpu.SemaphoreType.DMA
    hbm = pl.BlockSpec(memory_space=pltpu.HBM)
    return pl.pallas_call(
        functools.partial(kernel, n, nz, math.gcd(ctx, CHUNK)),
        out_shape=jax.ShapeDtypeStruct((count, cols), bf),
        in_specs=[hbm] * 5,
        out_specs=pl.BlockSpec(memory_space=pltpu.VMEM),
        scratch_shapes=[
            pltpu.VMEM((count, depth), bf),
            pltpu.VMEM((depth, width), bf),
            pltpu.VMEM((ctx, width), bf),
            pltpu.VMEM((ctx, width), bf),
            pltpu.VMEM(out_weight.shape, bf),
            pltpu.VMEM((width, ctx), bf),
            pltpu.VMEM((n, count, width), bf),
            pltpu.VMEM((ctx, 2 * count), f32),
            pltpu.VMEM((ctx, 2 * count), f32),
            pltpu.VMEM((n, width, count), bf),
            pltpu.VMEM((n, 8, count), f32),
            pltpu.VMEM((n, width, count), bf),
            pltpu.VMEM((n, 8, count), f32),
            pltpu.VMEM((nz, count, width), bf),
            pltpu.VMEM((nz, width, cols), bf),
            dma((5,)),
            dma((n,)), dma((n,)), dma((n,)), dma((n,)), dma((n,)), dma((n,)),
            dma((nz,)), dma((nz,)), dma((nz,)), dma((nz,)),
        ],
        compiler_params=pltpu.CompilerParams(
            collective_id=0, has_side_effects=True, vmem_limit_bytes=55136 * 1024),
    )(test_rows, query_weight, keys, values, out_weight)


def solution(mesh):
    in_specs = (
        P("rows", None),
        P(None, "heads"),
        P("rows", "heads"),
        P("rows", "heads"),
        P("heads", None),
    )
    body = functools.partial(shards, mesh.shape["rows"], mesh.shape["heads"])
    return jax.shard_map(body, mesh=mesh, in_specs=in_specs, out_specs=P("rows", "heads"), check_vma=False)
```

profile of v0, /device:TPU:0, one launch (start us, length us, event | category | flops | bytes accessed | tf_op | source)
XLA Modules:
  0.0 24.4 jit_solution(10526200984969719606)
XLA Ops:
  0.0 23.8 %shard_map.55 = bf16[128,128]{1,0:T(8,128)(2,1)S(1)} custom-call(bf16[128,512]{1,0:T(8,128)(2,1)} %x_hbm.1, bf16[512,128]{1,0:T(8,128)(2,1)} %wq_hbm.1, bf16[4096,128]{1,0:T(8,128)(2,1)} %k_hbm.1, bf16[4096,128]{1,0:T(8,128)(2,1)} %v_hbm.1, bf16[128,512]{1,0:T(8,128)(2,1)} %wo_hbm.1), custom_call_target="tpu_custom_call" | custom-call | tf_op jit(solution)/shard_map/pallas_call | solution.py:230
  23.8 0.6 %copy.7 = bf16[128,128]{1,0:T(8,128)(2,1)} copy(bf16[128,128]{1,0:T(8,128)(2,1)S(1)} %shard_map.55) | data formatting | bytes 65536
where the time goes:
time: 24.6 us; the launch traced here: 24.4 us
  Pallas kernels  23.8 us (97%)
  local copies, waits for them, and re-layouts  0.62 us (3%)
    pallas_call x1, Pallas kernels, shards(): pl.pallas_call(functools.partial(kernel, n, nz, math.gcd(ctx, CHUNK)), ou...  23.8 us
    unnamed x1, local copies, waits for them, and re-layouts  0.62 us

commit v1 on v0

--- a/solution.py
+++ b/solution.py
@@ -25,11 +25,23 @@
     return total
 
 
-def peer_of(me, step, count):
-    other = ((step - 1) * (step - 1) + count * count - 1) // (count * count)
-    early = ((count - 1 - step) * (count - 1 - step) + count * count - 1) // (count * count)
-    mask = other * early * (count + 1 - step) + 2 * (1 - other) + (1 - early)
-    return xor_of(me, mask, count)
+def near_masks(n):
+    return [m for m in range(1, n) if (m >> 1) & ((m >> 1) - 1) == 0]
+
+
+def turn_order(n):
+    near = near_masks(n)
+    far = [m for m in range(1, n) if m not in near]
+    return near[:3] + far + near[:2:-1]
+
+
+def peer_of(me, step, n):
+    if isinstance(step, int):
+        return xor_of(me, turn_order(n)[step - 1], n)
+    mask = 0
+    for i, m in enumerate(turn_order(n)):
+        mask = jnp.where(step == i + 1, m, mask)
+    return xor_of(me, mask, n)
 
 
 def kernel(
@@ -37,7 +49,7 @@
     x_hbm, wq_hbm, k_hbm, v_hbm, wo_hbm, o_ref,
     x_ref, wq_ref, k_ref, v_ref, wo_ref, vt_ref, qall, s0, s1,
     num_out, stat_out, num_in, stat_in, att, wo_in,
-    in_sem, q_send, q_recv, n_send, n_recv, t_send, t_recv, a_send, a_recv, w_send, w_recv,
+    in_sem, row_sem, col_sem, q_send, q_recv, n_send, n_recv, t_send, t_recv, a_send, a_recv, w_send, w_recv,
 ):
     me = lax.axis_index("rows")
     mz = lax.axis_index("heads")
@@ -54,19 +66,34 @@
     for load in loads:
         load.start()
 
+    near = near_masks(n)
+    below = (mz + nz - 1) // nz
+    above = (2 * nz - 2 - mz) // nz
+
+    def tell_columns(sem):
+        @pl.when(mz > 0)
+        def _():
+            pl.semaphore_signal(sem, inc=1, device_id={"heads": mz - 1}, device_id_type=MESH)
+
+        @pl.when(mz < nz - 1)
+        def _():
+            pl.semaphore_signal(sem, inc=1, device_id={"heads": mz + 1}, device_id_type=MESH)
+
+    def tell_rows(sem):
+        for m in spread_by:
+            pl.semaphore_signal(sem, inc=1, device_id={"rows": xor_of(me, m, n)}, device_id_type=MESH)
+
+    spread_by = [m for m in near if m > 1 and m % 2 == 0]
     barrier = pltpu.get_barrier_semaphore()
-    for i in range(1, n):
-        pl.semaphore_signal(barrier, inc=1, device_id={"rows": xor_of(me, i, n)}, device_id_type=MESH)
-    for i in range(1, nz):
-        pl.semaphore_signal(barrier, inc=1, device_id={"heads": (mz + i) % nz}, device_id_type=MESH)
+    for m in near:
+        pl.semaphore_signal(barrier, inc=1, device_id={"rows": xor_of(me, m, n)}, device_id_type=MESH)
+    tell_columns(barrier)
 
     loads[0].wait()
     loads[1].wait()
     q = jnp.dot(x_ref[...], wq_ref[...], preferred_element_type=f32).astype(bf)
     qall[me] = q * jnp.bfloat16(HEAD_DIM ** -0.5)
 
-    pl.semaphore_wait(barrier, n - 1 + nz - 1)
-
     def q_copy(peer, slot):
         return pltpu.make_async_remote_copy(
             src_ref=qall.at[me], dst_ref=qall.at[slot], send_sem=q_send.at[peer],
@@ -78,12 +105,6 @@
             src_ref=wo_ref.at[:, pl.ds(pl.multiple_of(peer * cols, cols), cols)],
             dst_ref=wo_in.at[mz], send_sem=w_send.at[i], recv_sem=w_recv.at[mz],
             device_id={"heads": peer}, device_id_type=MESH)
-
-    for i in range(1, n):
-        q_copy(peer_of(me, i, n), me).start()
-    loads[4].wait()
-    for i in range(1, nz):
-        w_copy(i).start()
 
     lane = lax.broadcasted_iota(jnp.int32, (1, width), 1)
     keep0 = jnp.where(lane < HEAD_DIM, 1.0, 0.0).astype(bf)
@@ -143,6 +164,15 @@
         return peer
 
     stat_out[...] = jnp.zeros(stat_out.shape, f32)
+    pl.semaphore_wait(barrier, len(near) + below + above)
+    if len(spread_by) > 1:
+        tell_rows(row_sem.at[0])
+    if nz > 2:
+        tell_columns(col_sem.at[0])
+    for m in turn_order(n):
+        if m in near:
+            q_copy(xor_of(me, m, n), me).start()
+
     loads[2].wait()
     loads[3].wait()
     both = both_heads(me)
@@ -151,18 +181,48 @@
         top = score(both, part, s0, top)
         vt_ref[:, part] = v_ref[part, :].T
 
-    top = turn(me, s0, top, await_q(1), s1)
+    for i in range(len(spread_by) - 1):
+        pl.semaphore_wait(row_sem.at[i], len(spread_by))
+        if i + 1 < len(spread_by) - 1:
+            tell_rows(row_sem.at[i + 1])
+    for m in turn_order(n):
+        if m not in near:
+            q_copy(xor_of(me, m, n), me).start()
+    for i in range(nz - 3):
+        pl.semaphore_wait(col_sem.at[i], below + above)
+        tell_columns(col_sem.at[i + 1])
+
+    turn(me, s0, top, None, None)
+
+    both = both_heads(await_q(1))
+    top = None
+    for part in chunks:
+        top = score(both, part, s1, top)
+
+    def share_weights():
+        if nz > 2:
+            pl.semaphore_wait(col_sem.at[nz - 3], below + above)
+        loads[4].wait()
+        for i in range(1, nz):
+            w_copy(i).start()
 
     def two(pair, top):
         step = 2 * pair + 1
         now, later = peer_of(me, step, n), await_q(step + 1)
         top = turn(now, s1, top, later, s0)
         send(now)
+
+        @pl.when(pair == 0)
+        def _():
+            share_weights()
+
         now, later = later, await_q(step + 2)
         top = turn(now, s0, top, later, s1)
         send(now)
         return top
 
+    if n == 2:
+        share_weights()
     top = lax.fori_loop(0, (n - 2) // 2, two, top)
     last = peer_of(me, n - 1, n)
     turn(last, s1, top, None, None)
@@ -249,6 +309,8 @@
             pltpu.VMEM((nz, count, width), bf),
             pltpu.VMEM((nz, width, cols), bf),
             dma((5,)),
+            pltpu.SemaphoreType.REGULAR((max(n.bit_length() - 3, 1),)),
+            pltpu.SemaphoreType.REGULAR((max(nz - 2, 1),)),
             dma((n,)), dma((n,)), dma((n,)), dma((n,)), dma((n,)), dma((n,)),
             dma((nz,)), dma((nz,)), dma((nz,)), dma((nz,)),
         ],

time: 24.6 us -> 24.4 us (level)
  no operation moved by 1% of the time
where the time goes in v1:
time: 24.4 us; the launch traced here: 24.3 us
  Pallas kernels  23.7 us (97%)
  local copies, waits for them, and re-layouts  0.62 us (3%)
    pallas_call x1, Pallas kernels, shards(): pl.pallas_call(functools.partial(kernel, n, nz, math.gcd(ctx, CHUNK)), ou...  23.7 us
    unnamed x1, local copies, waits for them, and re-layouts  0.62 us

profile of v1, /device:TPU:0, one launch (start us, length us, event | category | flops | bytes accessed | tf_op | source)
XLA Modules:
  0.0 24.3 jit_solution(166096322772990325)
XLA Ops:
  0.0 23.7 %shard_map.55 = bf16[128,128]{1,0:T(8,128)(2,1)S(1)} custom-call(bf16[128,512]{1,0:T(8,128)(2,1)} %x_hbm.1, bf16[512,128]{1,0:T(8,128)(2,1)} %wq_hbm.1, bf16[4096,128]{1,0:T(8,128)(2,1)} %k_hbm.1, bf16[4096,128]{1,0:T(8,128)(2,1)} %v_hbm.1, bf16[128,512]{1,0:T(8,128)(2,1)} %wo_hbm.1), custom_call_target="tpu_custom_call" | custom-call | tf_op jit(solution)/shard_map/pallas_call | solution.py:290
  23.7 0.6 %copy.7 = bf16[128,128]{1,0:T(8,128)(2,1)} copy(bf16[128,128]{1,0:T(8,128)(2,1)S(1)} %shard_map.55) | data formatting | bytes 65536

commit v2 on v1

--- a/solution.py
+++ b/solution.py
@@ -11,7 +11,7 @@
 HEAD_DIM = 64
 LOG2E = math.log2(math.e)
 MESH = pl.DeviceIdType.MESH
-CHUNK = 512
+CHUNK = 1024
 
 
 def xor_of(a, b, count):
@@ -120,11 +120,10 @@
         here = jnp.max(s, axis=0, keepdims=True)
         return here if top is None else jnp.maximum(top, here)
 
-    def weigh(s_ref, part, top, total, acc):
+    def weigh(s_ref, part, top, acc):
         w = jnp.exp2((s_ref[part, :] - top) * LOG2E)
-        here = jnp.sum(w, axis=0, keepdims=True)
         summed = jnp.dot(vt_ref[:, part], w.astype(bf), preferred_element_type=f32)
-        return (here, summed) if total is None else (total + here, acc + summed)
+        return summed if acc is None else acc + summed
 
     def keep(peer, top, total, acc):
         num = jnp.concatenate([acc[:HEAD_DIM, :count], acc[HEAD_DIM:, count:]], axis=0)
@@ -136,12 +135,12 @@
 
     def turn(now, s_now, top, later, s_later):
         both = None if later is None else both_heads(later)
-        after = total = acc = None
+        after = acc = None
         for part in chunks:
             if both is not None:
                 after = score(both, part, s_later, after)
-            total, acc = weigh(s_now, part, top, total, acc)
-        keep(now, top, total, acc)
+            acc = weigh(s_now, part, top, acc)
+        keep(now, top, acc[width:width + 1], acc[:width])
         return after
 
     def n_copy(peer, slot):
@@ -179,7 +178,8 @@
     top = None
     for part in chunks:
         top = score(both, part, s0, top)
-        vt_ref[:, part] = v_ref[part, :].T
+        vt_ref[:width, part] = v_ref[part, :].T
+        vt_ref[width:, part] = jnp.ones((16, chunk), bf)
 
     for i in range(len(spread_by) - 1):
         pl.semaphore_wait(row_sem.at[i], len(spread_by))
@@ -298,7 +298,7 @@
             pltpu.VMEM((ctx, width), bf),
             pltpu.VMEM((ctx, width), bf),
             pltpu.VMEM(out_weight.shape, bf),
-            pltpu.VMEM((width, ctx), bf),
+            pltpu.VMEM((width + 16, ctx), bf),
             pltpu.VMEM((n, count, width), bf),
             pltpu.VMEM((ctx, 2 * count), f32),
             pltpu.VMEM((ctx, 2 * count), f32),

time: 24.4 us -> 24.2 us (level)
  Pallas kernels: 23.7 us -> 23.4 us
    pallas_call x1, Pallas kernels: 23.7 us -> 23.4 us  [shards(): pl.pallas_call(functools.partial(kernel, n, nz, math.gcd(ctx, CHUNK)), ou...]
where the time goes in v2:
time: 24.2 us; the launch traced here: 24 us
  Pallas kernels  23.4 us (97%)
  local copies, waits for them, and re-layouts  0.62 us (3%)
    pallas_call x1, Pallas kernels, shards(): pl.pallas_call(functools.partial(kernel, n, nz, math.gcd(ctx, CHUNK)), ou...  23.4 us
    unnamed x1, local copies, waits for them, and re-layouts  0.62 us

profile of v2, /device:TPU:0, one launch (start us, length us, event | category | flops | bytes accessed | tf_op | source)
XLA Modules:
  0.0 24.0 jit_solution(15943590183023822307)
XLA Ops:
  0.0 23.4 %shard_map.55 = bf16[128,128]{1,0:T(8,128)(2,1)S(1)} custom-call(bf16[128,512]{1,0:T(8,128)(2,1)} %x_hbm.1, bf16[512,128]{1,0:T(8,128)(2,1)} %wq_hbm.1, bf16[4096,128]{1,0:T(8,128)(2,1)} %k_hbm.1, bf16[4096,128]{1,0:T(8,128)(2,1)} %v_hbm.1, bf16[128,512]{1,0:T(8,128)(2,1)} %wo_hbm.1), custom_call_target="tpu_custom_call" | custom-call | tf_op jit(solution)/shard_map/pallas_call | solution.py:290
  23.4 0.6 %copy.7 = bf16[128,128]{1,0:T(8,128)(2,1)} copy(bf16[128,128]{1,0:T(8,128)(2,1)S(1)} %shard_map.55) | data formatting | bytes 65536
